TPU v7x, 256 devices: a whole 4x4x8 slice. The times are simulated.
256 devices in a mesh: group: 8 (over y, x_lo), dom: 32 (over z, x_hi, core).
Axes of the slice: x: 4 (x_hi: 2, x_lo: 2; x = x_hi * 2 + x_lo), y: 4, z: 8, core: 2. Of those that a mesh axis runs over, the one named last changes fastest.
Arguments:
- feats: bfloat16 [524288, 128], P(('group', 'dom')), may hold values from -6 to 6
- coords: bfloat16 [3, 524288], P(None, ('group', 'dom')), may hold values from 0 to 1
- msg_cot: bfloat16 [524288, 128], P(('group', 'dom')), may hold values from -6 to 6
- send_list: int32 [256, 4, 2], P(('group', 'dom')), may hold values from 0 to 15
- tiles: int32 [256, 96, 2], P(('group', 'dom')), may hold values from 0 to 23, as said below
- tile_count: int32 [256], P(('group', 'dom')), may hold values from 24 to 96, as said below
- wavevec: int32 [512, 3], replicated, may hold values from -4 to 4
- w_rad_a: bfloat16 [128, 128], replicated, may hold values from -0.5 to 0.5
- w_rad_b: bfloat16 [128, 128], replicated, may hold values from -0.5 to 0.5
- w_charge: bfloat16 [128, 128], replicated, may hold values from -0.5 to 0.5
- w_long: bfloat16 [128, 128], replicated, may hold values from -0.5 to 0.5
- norm_gain: float32 [128], replicated, may hold values from 0.1 to 1.9
- w_in: bfloat16 [128, 256], replicated, may hold values from -0.5 to 0.5
- w_out: bfloat16 [256, 128], replicated, may hold values from -0.375 to 0.375
Outputs:
- new_feats: bfloat16 [524288, 128], P(('group', 'dom'))
- feat_adjoint: float32 [524288, 128], P(('group', 'dom'))
Inputs may be any that keep to these rules, and one draw needn't show every extreme that they name: In every domain the first 8 tiles have source blocks 16, 17, ... in order, one each; targets are below 16 and sources below 24. `tile_count`: tiles at or after a domain's count are not used; some domain has all 96 live.
All inputs are finite; a program needn't handle non-finite values.
Results may differ from a plain program's by a relative error of at most 0.0067.
Values may be sent and summed in bfloat16 or wider, within the bound.
A program may use at most 64 MiB of HBM per device.

v0:
```python
import jax
import jax.numpy as jnp
from jax import lax
from jax.sharding import PartitionSpec as P

BLK = 128
HB = 2
TILE_STEP = 16


RADIAL_A = 6.0
RADIAL_B = 30.0
MSG_SCALE = 1.0 / 32.0
EXACT = lax.Precision.HIGHEST


def shortened(shard):
    return jax.tree.map(lambda a: a.astype(jnp.bfloat16) if a.dtype == jnp.float32 else a, shard)


def passed_along(shard, axis, by):
    length = lax.axis_size(axis)
    return lax.ppermute(shard, axis, [(i, (i + by) % length) for i in range(length)])


def split_up(shard, dim, length):
    before, after = (shard.shape[:dim], shard.shape[dim + 1 :])
    return jnp.moveaxis(shard.reshape(*before, length, -1, *after), dim, 0)


def sum_at_owner(shard, axis, dim):
    length = lax.axis_size(axis)
    pieces = lax.all_to_all(split_up(shard, dim, length), axis, 0, 0, tiled=True)
    return jnp.sum(pieces, axis=0)


def in_order(pieces, dim):
    pieces = jnp.moveaxis(pieces, 0, dim)
    dims = pieces.shape
    return pieces.reshape(*dims[:dim], dims[dim] * dims[dim + 1], *dims[dim + 2 :])


def from_everyone(shard, axis):
    copies = jnp.broadcast_to(shard, (lax.axis_size(axis), *shard.shape))
    return lax.all_to_all(copies, axis, split_axis=0, concat_axis=0, tiled=True)


def collect(shard, axis, dim):
    return in_order(from_everyone(shard, axis), dim)


def along_dom(payload, offset):
    return jax.tree.map(
        lambda part, own: part.astype(own.dtype),
        passed_along(shortened(payload), "dom", offset),
        payload,
    )


def along_group(payload, offset):
    return jax.tree.map(
        lambda part, own: part.astype(own.dtype),
        passed_along(shortened(payload), "group", offset),
        payload,
    )


def back_dom(payload, offset):
    return passed_along(payload.astype(jnp.bfloat16), "dom", offset).astype(payload.dtype)


def back_group(payload, offset):
    return passed_along(payload.astype(jnp.bfloat16), "group", offset).astype(payload.dtype)


def selector(indices, length, dtype):
    return (indices[:, None] == jnp.arange(length, dtype=jnp.int32)[None, :]).astype(dtype)


def body(
    feats,
    coords,
    msg_cot,
    send_list,
    tiles,
    tile_count,
    wavevec,
    w_rad_a,
    w_rad_b,
    w_charge,
    w_long,
    norm_gain,
    w_in,
    w_out,
):
    atoms = feats.shape[0]
    width = feats.shape[1]
    nblk = atoms // BLK
    extent = nblk + 4 * HB
    blocks = feats.reshape(nblk, BLK, width)
    coord_blocks = coords.reshape(3, nblk, BLK)
    lists = send_list[0]
    sent = []
    for j in range(4):
        pick = selector(lists[j], nblk, jnp.bfloat16)
        sent_feats = jnp.einsum(
            "hn,nif->hif", pick, blocks, preferred_element_type=jnp.float32
        ).astype(jnp.bfloat16)
        sent_xyz = jnp.einsum(
            "hn,cni->chi", pick, coord_blocks, preferred_element_type=jnp.float32
        ).astype(jnp.bfloat16)
        sent.append((sent_feats, sent_xyz))
    got_first = along_dom(sent[0], 1)
    got_second = along_dom(sent[1], -1)
    got_third = along_group(sent[2], 1)
    got_fourth = along_group(sent[3], -1)
    wave = wavevec.astype(jnp.float32)
    norm2 = jnp.sum(wave * wave, axis=1)
    domains = lax.axis_size("dom")
    strength = jnp.exp(-norm2 / 16.0) / (1.0 + norm2) * float(atoms * domains) ** (-0.5)
    frac = coords.astype(jnp.float32)
    phase = (
        2.0
        * jnp.pi
        * (
            frac[0][:, None] * wave[:, 0][None, :]
            + frac[1][:, None] * wave[:, 1][None, :]
            + frac[2][:, None] * wave[:, 2][None, :]
        )
    )
    cos_t = jnp.cos(phase).astype(jnp.bfloat16)
    sin_t = jnp.sin(phase).astype(jnp.bfloat16)
    charges = jnp.dot(feats, w_charge, preferred_element_type=jnp.float32).astype(jnp.bfloat16)
    partial_struct = jnp.stack(
        [
            jnp.einsum("ak,ac->kc", cos_t, charges, preferred_element_type=jnp.float32),
            jnp.einsum("ak,ac->kc", sin_t, charges, preferred_element_type=jnp.float32),
        ]
    )
    share = sum_at_owner(partial_struct, "dom", 1)
    width_share = share.shape[1]
    strength_share = lax.dynamic_slice_in_dim(
        strength, lax.axis_index("dom") * width_share, width_share
    )
    weighted_share = (strength_share[None, :, None] * share).astype(jnp.bfloat16)
    weighted = collect(weighted_share, "dom", 1)
    potential = jnp.dot(cos_t, weighted[0], preferred_element_type=jnp.float32) + jnp.dot(
        sin_t, weighted[1], preferred_element_type=jnp.float32
    )
    long_msg = jnp.dot(potential.astype(jnp.bfloat16), w_long, preferred_element_type=jnp.float32)
    arrived = [got_first, got_second, got_third, got_fourth]
    ext_feats = jnp.concatenate([blocks] + [piece[0] for piece in arrived], axis=0)
    ext_xyz = jnp.concatenate([coord_blocks] + [piece[1] for piece in arrived], axis=1)
    flat = ext_feats.reshape(extent * BLK, width)
    proj_a = (
        jnp.dot(flat, w_rad_a, preferred_element_type=jnp.float32)
        .astype(jnp.bfloat16)
        .reshape(extent, BLK, width)
    )
    proj_b = (
        jnp.dot(flat, w_rad_b, preferred_element_type=jnp.float32)
        .astype(jnp.bfloat16)
        .reshape(extent, BLK, width)
    )
    cot_blocks = msg_cot.reshape(nblk, BLK, width)
    slots = tiles.shape[1]
    count = tile_count[0]
    target_all = tiles[0, :, 0]
    source_all = tiles[0, :, 1]
    live_all = (jnp.arange(slots) < count).astype(jnp.float32)

    def tile_work(carry, first):
        msg, grad_a, grad_b = carry
        target = lax.dynamic_slice_in_dim(target_all, first, TILE_STEP)
        source = lax.dynamic_slice_in_dim(source_all, first, TILE_STEP)
        live = lax.dynamic_slice_in_dim(live_all, first, TILE_STEP)
        pick_t = selector(target, nblk, jnp.bfloat16)
        pick_s = selector(source, extent, jnp.bfloat16)
        put_t = selector(target, nblk, jnp.float32) * live[:, None]
        put_s = selector(source, extent, jnp.float32) * live[:, None]
        near = jnp.einsum("sn,cni->sci", pick_t, coord_blocks, preferred_element_type=jnp.float32)
        far = jnp.einsum("se,cej->scj", pick_s, ext_xyz, preferred_element_type=jnp.float32)
        diff = near[:, :, :, None] - far[:, :, None, :]
        dist2 = jnp.sum(diff * diff, axis=1)
        ker_a = jnp.exp(-RADIAL_A * dist2).astype(jnp.bfloat16)
        ker_b = jnp.exp(-RADIAL_B * dist2).astype(jnp.bfloat16)
        src_a = jnp.einsum(
            "se,ejf->sjf", pick_s, proj_a, preferred_element_type=jnp.float32
        ).astype(jnp.bfloat16)
        src_b = jnp.einsum(
            "se,ejf->sjf", pick_s, proj_b, preferred_element_type=jnp.float32
        ).astype(jnp.bfloat16)
        term = jnp.einsum("sij,sjf->sif", ker_a, src_a, preferred_element_type=jnp.float32)
        term = term + jnp.einsum("sij,sjf->sif", ker_b, src_b, preferred_element_type=jnp.float32)
        msg = msg + jnp.einsum("sn,sif->nif", put_t, term, precision=EXACT)
        cot_tiles = jnp.einsum(
            "sn,nif->sif", pick_t, cot_blocks, preferred_element_type=jnp.float32
        ).astype(jnp.bfloat16)
        back_a = jnp.einsum("sij,sif->sjf", ker_a, cot_tiles, preferred_element_type=jnp.float32)
        back_b = jnp.einsum("sij,sif->sjf", ker_b, cot_tiles, preferred_element_type=jnp.float32)
        grad_a = grad_a + jnp.einsum("se,sjf->ejf", put_s, back_a, precision=EXACT)
        grad_b = grad_b + jnp.einsum("se,sjf->ejf", put_s, back_b, precision=EXACT)
        return (msg, grad_a, grad_b)

    def tile_step(carry, index):
        first = index * TILE_STEP
        carry = lax.cond(first < count, lambda c: tile_work(c, first), lambda c: c, carry)
        return (carry, None)

    start = (
        jnp.zeros((nblk, BLK, width), jnp.float32),
        jnp.zeros((extent, BLK, width), jnp.float32),
        jnp.zeros((extent, BLK, width), jnp.float32),
    )
    (msg, grad_a, grad_b), unused = lax.scan(
        tile_step, start, jnp.arange(slots // TILE_STEP, dtype=jnp.int32)
    )
    msg = MSG_SCALE * msg
    grad_a = (MSG_SCALE * grad_a).astype(jnp.bfloat16).reshape(extent * BLK, width)
    grad_b = (MSG_SCALE * grad_b).astype(jnp.bfloat16).reshape(extent * BLK, width)
    grad_ext = jnp.dot(grad_a, w_rad_a.T, preferred_element_type=jnp.float32) + jnp.dot(
        grad_b, w_rad_b.T, preferred_element_type=jnp.float32
    )
    grad_ext = grad_ext.reshape(extent, BLK, width)
    held = grad_ext[nblk:]
    returned = jnp.concatenate(
        [
            back_dom(held[0:HB], -1),
            back_dom(held[HB : 2 * HB], 1),
            back_group(held[2 * HB : 3 * HB], -1),
            back_group(held[3 * HB : 4 * HB], 1),
        ],
        axis=0,
    )
    place = selector(lists.reshape(-1), nblk, jnp.float32)
    adjoint = grad_ext[:nblk] + jnp.einsum("hn,hif->nif", place, returned, precision=EXACT)
    mixed = feats.astype(jnp.float32) + msg.reshape(atoms, width) + long_msg
    scale = lax.rsqrt(jnp.mean(mixed * mixed, axis=1, keepdims=True) + 1e-06)
    normed = (mixed * scale * norm_gain[None, :]).astype(jnp.bfloat16)
    hidden = jax.nn.silu(jnp.dot(normed, w_in, preferred_element_type=jnp.float32)).astype(
        jnp.bfloat16
    )
    new_feats = (mixed + jnp.dot(hidden, w_out, preferred_element_type=jnp.float32)).astype(
        jnp.bfloat16
    )
    return (new_feats, adjoint.reshape(atoms, width))


def solution(mesh):
    return jax.shard_map(
        body,
        mesh=mesh,
        in_specs=(
            P(("group", "dom"), None),
            P(None, ("group", "dom")),
            P(("group", "dom"), None),
            P(("group", "dom"), None, None),
            P(("group", "dom"), None, None),
            P(("group", "dom")),
            P(),
            P(),
            P(),
            P(),
            P(),
            P(),
            P(),
            P(),
        ),
        out_specs=(P(("group", "dom"), None), P(("group", "dom"), None)),
        check_vma=False,
    )
```

profile of v0, /device:TPU:1, one launch (start us, length us, event | category | flops | bytes accessed | tf_op | source)
XLA Modules:
  0.0 239.0 jit_solution(4750016212759522038)
XLA Ops:
  2.6 4.1 %collective-permute-start = (bf16[3,2,128]{2,1,0:T(2,128)(2,1)S(1)}, bf16[3,2,128]{2,1,0:T(2,128)(2,1)S(1)}, u32[]{:S(2)}, u32[]{:S(2)}) collective-permute-start(bf16[3,2,128]{2,1,0:T(2,128)(2,1)S(1)} %fusion.55), channel_id=1, source_target_pairs={{0,1},{1,2},{2,3},{3,4},{4,5},{5,6},{6,7},{7,8},{8,9},{9,10},{10,1... | collective-permute-start | bytes 4616 | tf_op jit(solution)/shard_map/ppermute | solution.py:23
  7.6 3.3 %collective-permute-start.3 = (bf16[3,2,128]{2,1,0:T(2,128)(2,1)S(1)}, bf16[3,2,128]{2,1,0:T(2,128)(2,1)S(1)}, u32[]{:S(2)}, u32[]{:S(2)}) collective-permute-start(bf16[3,2,128]{2,1,0:T(2,128)(2,1)S(1)} %fusion.58), channel_id=1, source_target_pairs={{0,224},{32,0},{64,32},{96,64},{128,96},{160,128},{192,160},{224,1... | collective-permute-start | bytes 4616 | tf_op jit(solution)/shard_map/ppermute | solution.py:23
  12.4 4.1 %collective-permute-start.4 = (bf16[2,128,128]{2,0,1:T(2,128)(2,1)S(1)}, bf16[2,128,128]{2,0,1:T(2,128)(2,1)S(1)}, u32[]{:S(2)}, u32[]{:S(2)}) collective-permute-start(bf16[2,128,128]{2,0,1:T(2,128)(2,1)S(1)} %convolution_convert_fusion.9), channel_id=1, source_target_pairs={{0,1},{1,2},{2,3},{3,4},{4,5},{5,6},{6,7},{7,8},{8,9},{9,10},{10,1... | collective-permute-start | bytes 196616 | tf_op jit(solution)/shard_map/ppermute | solution.py:23
  19.3 15.5 %fusion.54 = f32[512,128]{1,0:T(8,128)S(1)} fusion(bf16[2048,128]{1,0:T(8,128)(2,1)S(1)} %convolution_convert_fusion.5, f32[512]{0:T(512)S(1)} %bitcast.170, f32[2048]{0:T(1024)S(1)} %bitcast.162, f32[512]{0:T(512)S(1)} %bitcast.174, f32[2048]{0:T(1024)S(1)} %bitcast.158, f32[512]{0:T(512)S(1)} %bitcast.166, f32[2048]{0:T(1024)S(1)} %bitcast.154), kind=kOutput, calls=%fused_computation.74 | convolution fusion | flops 275775488 | bytes 817152 | tf_op jit(solution)/shard_map/ak,ac->kc/dot_general | solution.py:136
  34.9 15.3 %fusion.52 = f32[512,128]{1,0:T(8,128)S(1)} fusion(bf16[2048,128]{1,0:T(8,128)(2,1)S(1)} %convolution_convert_fusion.5, f32[512]{0:T(512)S(1)} %bitcast.171, f32[2048]{0:T(1024)S(1)} %bitcast.163, f32[512]{0:T(512)S(1)} %bitcast.175, f32[2048]{0:T(1024)S(1)} %bitcast.159, f32[512]{0:T(512)S(1)} %bitcast.167, f32[2048]{0:T(1024)S(1)} %bitcast.155), kind=kOutput, calls=%fused_computation.72 | convolution fusion | flops 275775488 | bytes 817152 | tf_op jit(solution)/shard_map/ak,ac->kc/dot_general | solution.py:137
  51.1 11.0 %all-to-all-start = ((f32[32,2,16,128]{3,2,1,0:T(8,128)}), f32[32,2,16,128]{3,2,1,0:T(8,128)}, u32[]{:S(2)}, u32[]{:S(2)}) async-start(f32[32,2,16,128]{3,2,1,0:T(8,128)} %maximum_bitcast_fusion), calls=%async_computation | async-start | bytes 1048576 | tf_op jit(solution)/shard_map/all_to_all | solution.py:33
  66.2 4.0 %collective-permute-start.7 = (bf16[2,128,128]{2,0,1:T(2,128)(2,1)S(1)}, bf16[2,128,128]{2,0,1:T(2,128)(2,1)S(1)}, u32[]{:S(2)}, u32[]{:S(2)}) collective-permute-start(bf16[2,128,128]{2,0,1:T(2,128)(2,1)S(1)} %convolution_convert_fusion.6), channel_id=1, source_target_pairs={{0,224},{32,0},{64,32},{96,64},{128,96},{160,128},{192,160},{224,1... | collective-permute-start | bytes 196616 | tf_op jit(solution)/shard_map/ppermute | solution.py:23
  70.2 3.1 %collective-permute-done.5 = bf16[2,128,128]{2,0,1:T(2,128)(2,1)S(1)} collective-permute-done((bf16[2,128,128]{2,0,1:T(2,128)(2,1)S(1)}, bf16[2,128,128]{2,0,1:T(2,128)(2,1)S(1)}, u32[]{:S(2)}, u32[]{:S(2)}) %collective-permute-start.5) | collective-permute-done | bytes 65568 | tf_op jit(solution)/shard_map/ppermute | solution.py:23
  78.2 65.5 %while.16 = (s32[]{:T(128)}, f32[16,128,128]{2,0,1:T(8,128)}, f32[24,128,128]{2,0,1:T(8,128)S(1)}, f32[24,128,128]{2,0,1:T(8,128)S(1)}, s32[6]{0:T(128)S(1)}, /*...) while((s32[]{:T(128)}, f32[16,128,128]{2,0,1:T(8,128)}, ...), condition=%wide.region_4.5_spmd.clone.clone, body=%wide.region_0.4_spmd.clone.clone.sunk | while | flops 510103360 | bytes 44793800 | solution.py:215
  80.6 12.7 %conditional.4 = ((f32[16,128,128]{2,0,1:T(8,128)}, f32[24,128,128]{2,0,1:T(8,128)S(1)}, f32[24,128,128]{2,0,1:T(8,128)S(1)})) conditional(s32[]{:T(128)} %convert_element_type.229, (f32[16,128,128]{2,0,1:T(8,128)}, f32[24,128,128]{2,0,1:T(8,128)S(1)}, f32[24,128,128]{2,0,1:T(8,128)S(1)}) %tuple.63, (s32[]{:T(128)}, s32[96]{0:T(128)S(1)}, ...), branch_computations={%region_1.1_spmd, %region_2.3_spmd} | conditional | flops 510103168 | bytes 44793112 | solution.py:207
  88.2 2.4 convolution_add_fusion
  90.9 2.4 convolution_add_fusion.1
  95.8 12.7 %conditional.4 = ((f32[16,128,128]{2,0,1:T(8,128)}, f32[24,128,128]{2,0,1:T(8,128)S(1)}, f32[24,128,128]{2,0,1:T(8,128)S(1)})) conditional(s32[]{:T(128)} %convert_element_type.229, (f32[16,128,128]{2,0,1:T(8,128)}, f32[24,128,128]{2,0,1:T(8,128)S(1)}, f32[24,128,128]{2,0,1:T(8,128)S(1)}) %tuple.63, (s32[]{:T(128)}, s32[96]{0:T(128)S(1)}, ...), branch_computations={%region_1.1_spmd, %region_2.3_spmd} | conditional | flops 510103168 | bytes 44793112 | solution.py:207
  106.1 2.4 convolution_add_fusion.1
  110.9 12.7 %conditional.4 = ((f32[16,128,128]{2,0,1:T(8,128)}, f32[24,128,128]{2,0,1:T(8,128)S(1)}, f32[24,128,128]{2,0,1:T(8,128)S(1)})) conditional(s32[]{:T(128)} %convert_element_type.229, (f32[16,128,128]{2,0,1:T(8,128)}, f32[24,128,128]{2,0,1:T(8,128)S(1)}, f32[24,128,128]{2,0,1:T(8,128)S(1)}) %tuple.63, (s32[]{:T(128)}, s32[96]{0:T(128)S(1)}, ...), branch_computations={%region_1.1_spmd, %region_2.3_spmd} | conditional | flops 510103168 | bytes 44793112 | solution.py:207
  121.3 2.4 convolution_add_fusion.1
  126.1 12.7 %conditional.4 = ((f32[16,128,128]{2,0,1:T(8,128)}, f32[24,128,128]{2,0,1:T(8,128)S(1)}, f32[24,128,128]{2,0,1:T(8,128)S(1)})) conditional(s32[]{:T(128)} %convert_element_type.229, (f32[16,128,128]{2,0,1:T(8,128)}, f32[24,128,128]{2,0,1:T(8,128)S(1)}, f32[24,128,128]{2,0,1:T(8,128)S(1)}) %tuple.63, (s32[]{:T(128)}, s32[96]{0:T(128)S(1)}, ...), branch_computations={%region_1.1_spmd, %region_2.3_spmd} | conditional | flops 510103168 | bytes 44793112 | solution.py:207
  136.4 2.4 convolution_add_fusion.1
  147.0 4.4 %collective-permute-start.8 = (bf16[2,128,128]{2,0,1:T(2,128)(2,1)S(1)}, bf16[2,128,128]{2,0,1:T(2,128)(2,1)S(1)}, u32[]{:S(2)}, u32[]{:S(2)}) collective-permute-start(bf16[2,128,128]{2,0,1:T(2,128)(2,1)S(1)} %copy.131), channel_id=1, source_target_pairs={{0,31},{1,0},{2,1},{3,2},{4,3},{5,4},{6,5},{7,6},{8,7},{9,8},{10,9... | collective-permute-start | bytes 196616 | tf_op jit(solution)/shard_map/ppermute | solution.py:23
  153.5 36.9 %all-to-all-start.1 = ((bf16[32,2,16,128]{3,2,1,0:T(8,128)(2,1)}), bf16[32,2,16,128]{3,2,1,0:T(8,128)(2,1)S(1)}, u32[]{:S(2)}, u32[]{:S(2)}) async-start(bf16[32,2,16,128]{3,2,1,0:T(8,128)(2,1)} %broadcast_in_dim.5), calls=%async_computation.1 | async-start | bytes 524288 | tf_op jit(solution)/shard_map/all_to_all | solution.py:45
  195.7 7.5 %all-to-all-done.1 = bf16[32,2,16,128]{3,2,1,0:T(8,128)(2,1)S(1)} async-done(((bf16[32,2,16,128]{3,2,1,0:T(8,128)(2,1)}), bf16[32,2,16,128]{3,2,1,0:T(8,128)(2,1)S(1)}, u32[]{:S(2)}, u32[]{:S(2)}) %all-to-all-start.1) | async-done | bytes 262176 | tf_op jit(solution)/shard_map/all_to_all | solution.py:45
  203.2 15.1 %fusion.53 = f32[2048,128]{1,0:T(8,128)S(1)} fusion(bf16[512,128]{1,0:T(8,128)(2,1)S(1)} %bitcast.146, f32[512]{0:T(512)S(1)} %bitcast.172, f32[2048]{0:T(1024)S(1)} %bitcast.164, f32[512]{0:T(512)S(1)} %bitcast.176, f32[2048]{0:T(1024)S(1)} %bitcast.160, f32[512]{0:T(512)S(1)} %bitcast.168, f32[2048]{0:T(1024)S(1)} %bitcast.156), kind=kOutput, calls=%fused_computation.73 | convolution fusion | flops 275775488 | bytes 1210368 | tf_op jit(solution)/shard_map/dot_general | solution.py:147
  218.4 16.6 %multiply_reduce_fusion.1 = (f32[2048]{0:T(1024)S(1)}, f32[2048,128]{0,1:T(8,128)}) fusion(bf16[128,128]{1,0:T(8,128)(2,1)S(1)} %copy-done.16, f32[2048,128]{1,0:T(8,128)S(1)} %fusion.53, bf16[512,128]{1,0:T(8,128)(2,1)S(1)} %bitcast.145, f32[512]{0:T(512)S(1)} %bitcast.173, f32[2048]{0:T(1024)S(1)} %bitcast.165, f32[512]{0:T(512)S(1)} %bitcast.177, ...), kind=kOutput, calls=%fused_computation.91 | convolution fusion | flops 344717312 | bytes 3872768 | tf_op jit(solution)/shard_map/dot_general | solution.py:150
  235.0 2.5 %fusion.48 = bf16[2048,128]{0,1:T(8,128)(2,1)S(1)} fusion(f32[2048,128]{0,1:T(8,128)} %get-tuple-element.283, bf16[256,128]{1,0:T(8,128)(2,1)S(1)} %copy-done, bf16[128,256]{1,0:T(8,128)(2,1)S(1)} %copy-done.15, f32[128]{0:T(128)S(1)} %copy-done.17, f32[2048]{0:T(1024)S(1)} %add_rsqrt_fusion), kind=kOutput, calls=%fused_computation.64 | convolution fusion | flops 272367616 | bytes 1712640 | tf_op jit(solution)/shard_map/dot_general | solution.py:243
  (222 shorter events, 74.3 us)
Async XLA Ops:
  0.6 234.4 %copy-start = (bf16[256,128]{1,0:T(8,128)(2,1)S(1)}, bf16[256,128]{1,0:T(8,128)(2,1)}, u32[]{:S(2)}) copy-start(bf16[256,128]{1,0:T(8,128)(2,1)} %param.31) | copy-start | bytes 196612
  2.6 63.2 %collective-permute-start = (bf16[3,2,128]{2,1,0:T(2,128)(2,1)S(1)}, bf16[3,2,128]{2,1,0:T(2,128)(2,1)S(1)}, u32[]{:S(2)}, u32[]{:S(2)}) collective-permute-start(bf16[3,2,128]{2,1,0:T(2,128)(2,1)S(1)} %fusion.55), channel_id=1, source_target_pairs={{0,1},{1,2},{2,3},{3,4},{4,5},{5,6},{6,7},{7,8},{8,9},{9,10},{10,1... | collective-permute-start | bytes 4616 | tf_op jit(solution)/shard_map/ppermute | solution.py:23
  6.9 59.2 %collective-permute-start.1 = (bf16[3,2,128]{2,1,0:T(2,128)(2,1)S(1)}, bf16[3,2,128]{2,1,0:T(2,128)(2,1)S(1)}, u32[]{:S(2)}, u32[]{:S(2)}) collective-permute-start(bf16[3,2,128]{2,1,0:T(2,128)(2,1)S(1)} %fusion.56), channel_id=1, source_target_pairs={{0,31},{1,0},{2,1},{3,2},{4,3},{5,4},{6,5},{7,6},{8,7},{9,8},{10,9... | collective-permute-start | bytes 4616 | tf_op jit(solution)/shard_map/ppermute | solution.py:23
  7.1 59.0 %collective-permute-start.2 = (bf16[3,2,128]{2,1,0:T(2,128)(2,1)S(1)}, bf16[3,2,128]{2,1,0:T(2,128)(2,1)S(1)}, u32[]{:S(2)}, u32[]{:S(2)}) collective-permute-start(bf16[3,2,128]{2,1,0:T(2,128)(2,1)S(1)} %fusion.57), channel_id=1, source_target_pairs={{0,32},{32,64},{64,96},{96,128},{128,160},{160,192},{192,224},{224... | collective-permute-start | bytes 4616 | tf_op jit(solution)/shard_map/ppermute | solution.py:23
  7.6 62.5 %collective-permute-start.3 = (bf16[3,2,128]{2,1,0:T(2,128)(2,1)S(1)}, bf16[3,2,128]{2,1,0:T(2,128)(2,1)S(1)}, u32[]{:S(2)}, u32[]{:S(2)}) collective-permute-start(bf16[3,2,128]{2,1,0:T(2,128)(2,1)S(1)} %fusion.58), channel_id=1, source_target_pairs={{0,224},{32,0},{64,32},{96,64},{128,96},{160,128},{192,160},{224,1... | collective-permute-start | bytes 4616 | tf_op jit(solution)/shard_map/ppermute | solution.py:23
  12.4 57.8 %collective-permute-start.4 = (bf16[2,128,128]{2,0,1:T(2,128)(2,1)S(1)}, bf16[2,128,128]{2,0,1:T(2,128)(2,1)S(1)}, u32[]{:S(2)}, u32[]{:S(2)}) collective-permute-start(bf16[2,128,128]{2,0,1:T(2,128)(2,1)S(1)} %convolution_convert_fusion.9), channel_id=1, source_target_pairs={{0,1},{1,2},{2,3},{3,4},{4,5},{5,6},{6,7},{7,8},{8,9},{9,10},{10,1... | collective-permute-start | bytes 196616 | tf_op jit(solution)/shard_map/ppermute | solution.py:23
  50.2 11.8 %copy-start.6 = (bf16[2048,128]{1,0:T(8,128)(2,1)S(1)}, bf16[2048,128]{1,0:T(8,128)(2,1)}, u32[]{:S(2)}) copy-start(bf16[2048,128]{1,0:T(8,128)(2,1)} %param.18) | copy-start | bytes 1572868
  51.1 12.3 %copy-start.12 = (s32[512,3]{0,1:T(4,128)S(1)}, s32[512,3]{0,1:T(4,128)}, u32[]{:S(2)}) copy-start(s32[512,3]{0,1:T(4,128)} %param.24) | copy-start | bytes 18436
  51.1 12.3 %copy-start.14 = (s32[1,96,2]{1,2,0:T(2,128)S(1)}, s32[1,96,2]{1,2,0:T(2,128)}, u32[]{:S(2)}) copy-start(s32[1,96,2]{1,2,0:T(2,128)} %param.22) | copy-start | bytes 2308
  51.1 100.5 %all-to-all-start = ((f32[32,2,16,128]{3,2,1,0:T(8,128)}), f32[32,2,16,128]{3,2,1,0:T(8,128)}, u32[]{:S(2)}, u32[]{:S(2)}) async-start(f32[32,2,16,128]{3,2,1,0:T(8,128)} %maximum_bitcast_fusion), calls=%async_computation | async-start | bytes 1048576 | tf_op jit(solution)/shard_map/all_to_all | solution.py:33
  63.4 9.9 %copy-start.10 = (bf16[128,128]{1,0:T(8,128)(2,1)S(1)}, bf16[128,128]{1,0:T(8,128)(2,1)}, u32[]{:S(2)}) copy-start(bf16[128,128]{1,0:T(8,128)(2,1)} %param.25) | copy-start | bytes 98308
  65.8 7.4 %collective-permute-start.5 = (bf16[2,128,128]{2,0,1:T(2,128)(2,1)S(1)}, bf16[2,128,128]{2,0,1:T(2,128)(2,1)S(1)}, u32[]{:S(2)}, u32[]{:S(2)}) collective-permute-start(bf16[2,128,128]{2,0,1:T(2,128)(2,1)S(1)} %convolution_convert_fusion.8), channel_id=1, source_target_pairs={{0,31},{1,0},{2,1},{3,2},{4,3},{5,4},{6,5},{7,6},{8,7},{9,8},{10,9... | collective-permute-start | bytes 196616 | tf_op jit(solution)/shard_map/ppermute | solution.py:23
  66.2 7.1 %collective-permute-start.6 = (bf16[2,128,128]{2,0,1:T(2,128)(2,1)S(1)}, bf16[2,128,128]{2,0,1:T(2,128)(2,1)S(1)}, u32[]{:S(2)}, u32[]{:S(2)}) collective-permute-start(bf16[2,128,128]{2,0,1:T(2,128)(2,1)S(1)} %convolution_convert_fusion.7), channel_id=1, source_target_pairs={{0,32},{32,64},{64,96},{96,128},{128,160},{160,192},{192,224},{224... | collective-permute-start | bytes 196616 | tf_op jit(solution)/shard_map/ppermute | solution.py:23
  66.2 7.2 %collective-permute-start.7 = (bf16[2,128,128]{2,0,1:T(2,128)(2,1)S(1)}, bf16[2,128,128]{2,0,1:T(2,128)(2,1)S(1)}, u32[]{:S(2)}, u32[]{:S(2)}) collective-permute-start(bf16[2,128,128]{2,0,1:T(2,128)(2,1)S(1)} %convolution_convert_fusion.6), channel_id=1, source_target_pairs={{0,224},{32,0},{64,32},{96,64},{128,96},{160,128},{192,160},{224,1... | collective-permute-start | bytes 196616 | tf_op jit(solution)/shard_map/ppermute | solution.py:23
  145.2 45.2 %copy-start.3 = (f32[16,128,128]{2,0,1:T(8,128)S(1)}, f32[16,128,128]{2,0,1:T(8,128)}, u32[]{:S(2)}) copy-start(f32[16,128,128]{2,0,1:T(8,128)} %get-tuple-element.121) | copy-start | bytes 3145732
  145.3 48.1 %collective-permute-start.10 = (bf16[2,128,128]{2,0,1:T(2,128)(2,1)S(1)}, bf16[2,128,128]{2,0,1:T(2,128)(2,1)S(1)}, u32[]{:S(2)}, u32[]{:S(2)}) collective-permute-start(bf16[2,128,128]{2,0,1:T(2,128)(2,1)S(1)} %copy.133), channel_id=1, source_target_pairs={{0,224},{32,0},{64,32},{96,64},{128,96},{160,128},{192,160},{224,1... | collective-permute-start | bytes 196616 | tf_op jit(solution)/shard_map/ppermute | solution.py:23
  145.4 47.9 %collective-permute-start.11 = (bf16[2,128,128]{2,0,1:T(2,128)(2,1)S(1)}, bf16[2,128,128]{2,0,1:T(2,128)(2,1)S(1)}, u32[]{:S(2)}, u32[]{:S(2)}) collective-permute-start(bf16[2,128,128]{2,0,1:T(2,128)(2,1)S(1)} %copy.134), channel_id=1, source_target_pairs={{0,32},{32,64},{64,96},{96,128},{128,160},{160,192},{192,224},{224... | collective-permute-start | bytes 196616 | tf_op jit(solution)/shard_map/ppermute | solution.py:23
  147.0 46.4 %collective-permute-start.8 = (bf16[2,128,128]{2,0,1:T(2,128)(2,1)S(1)}, bf16[2,128,128]{2,0,1:T(2,128)(2,1)S(1)}, u32[]{:S(2)}, u32[]{:S(2)}) collective-permute-start(bf16[2,128,128]{2,0,1:T(2,128)(2,1)S(1)} %copy.131), channel_id=1, source_target_pairs={{0,31},{1,0},{2,1},{3,2},{4,3},{5,4},{6,5},{7,6},{8,7},{9,8},{10,9... | collective-permute-start | bytes 196616 | tf_op jit(solution)/shard_map/ppermute | solution.py:23
  151.5 41.9 %collective-permute-start.9 = (bf16[2,128,128]{2,0,1:T(2,128)(2,1)S(1)}, bf16[2,128,128]{2,0,1:T(2,128)(2,1)S(1)}, u32[]{:S(2)}, u32[]{:S(2)}) collective-permute-start(bf16[2,128,128]{2,0,1:T(2,128)(2,1)S(1)} %copy.132), channel_id=1, source_target_pairs={{0,1},{1,2},{2,3},{3,4},{4,5},{5,6},{6,7},{7,8},{8,9},{9,10},{10,1... | collective-permute-start | bytes 196616 | tf_op jit(solution)/shard_map/ppermute | solution.py:23
  153.5 49.7 %all-to-all-start.1 = ((bf16[32,2,16,128]{3,2,1,0:T(8,128)(2,1)}), bf16[32,2,16,128]{3,2,1,0:T(8,128)(2,1)S(1)}, u32[]{:S(2)}, u32[]{:S(2)}) async-start(bf16[32,2,16,128]{3,2,1,0:T(8,128)(2,1)} %broadcast_in_dim.5), calls=%async_computation.1 | async-start | bytes 524288 | tf_op jit(solution)/shard_map/all_to_all | solution.py:45
  203.2 15.1 %copy-start.9 = (bf16[2048,128]{0,1:T(8,128)(2,1)S(1)}, bf16[2048,128]{0,1:T(8,128)(2,1)}, u32[]{:S(2)}) copy-start(bf16[2048,128]{0,1:T(8,128)(2,1)} %copy.112) | copy-start | bytes 1572868
  203.2 15.1 %copy-start.16 = (bf16[128,128]{1,0:T(8,128)(2,1)S(1)}, bf16[128,128]{1,0:T(8,128)(2,1)}, u32[]{:S(2)}) copy-start(bf16[128,128]{1,0:T(8,128)(2,1)} %param.28) | copy-start | bytes 98308
  218.3 16.7 %copy-start.15 = (bf16[128,256]{1,0:T(8,128)(2,1)S(1)}, bf16[128,256]{1,0:T(8,128)(2,1)}, u32[]{:S(2)}) copy-start(bf16[128,256]{1,0:T(8,128)(2,1)} %param.30) | copy-start | bytes 196612
  218.3 16.7 %copy-start.17 = (f32[128]{0:T(128)S(1)}, f32[128]{0:T(128)}, u32[]{:S(2)}) copy-start(f32[128]{0:T(128)} %param.29) | copy-start | bytes 1540
  (23 other events, 32.5 us)
where the time goes:
time: 244 us; the launch traced here: 239 us
  matrix products  110 us (45%)
  starting transfers between devices  70 us (29%)
  local copies, waits for them, and re-layouts  26.1 us (11%)
  other arithmetic  12.5 us (5%)
  waiting for transfers between devices  10.6 us (4%)
  loops' own time  8.02 us (3%)
    all_to_all x1, starting transfers between devices, from_everyone(): return lax.all_to_all(copies, axis, split_axis=0, concat_axis=0, tiled=True)  36.9 us
    ppermute x12, starting transfers between devices, passed_along(): lax.ppermute(shard, axis, [(i, (i + by) % length) for i in range(length)])  22.1 us
    dot_general x1, matrix products, body(): jnp.dot(potential.astype(jnp.bfloat16), w_long, preferred_element_type=jn...  16.6 us
    dot_general x1, matrix products, body(): jnp.einsum('ak,ac->kc', cos_t, charges, preferred_element_type=jnp.float32)  15.5 us
    dot_general x1, matrix products, body(): jnp.einsum('ak,ac->kc', sin_t, charges, preferred_element_type=jnp.float32)  15.3 us
    dot_general x1, matrix products, body(): jnp.dot(cos_t, weighted[0], preferred_element_type=jnp.float32)  15.1 us
    all_to_all x1, starting transfers between devices, sum_at_owner(): lax.all_to_all(split_up(shard, dim, length), axis, 0, 0, tiled=True)  11 us
    dot_general x4, matrix products, tile_work(): grad_a = grad_a + jnp.einsum('se,sjf->ejf', put_s, back_a, precision=EXACT)  9.52 us
  transfers between devices with their start and end apart: 14, of which 2 were waited for; matrix products, arithmetic and copies ran while one was open for 44% of the time, Pallas kernels for 0%

commit v1 on v0

v1 whole, which is shorter than its diff:
```python
import functools

import jax
import jax.numpy as jnp
from jax import lax
from jax.experimental import pallas as pl
from jax.experimental.pallas import tpu as pltpu
from jax.sharding import PartitionSpec as P

BLK = 128
F = 128
HB = 2
MESH = pl.DeviceIdType.MESH
F32 = jnp.float32
BF16 = jnp.bfloat16
SCALE = 1.0 / 32.0
LOG2E = 1.4426950408889634
SIN_C = (4.44288292, -7.30824569, 3.60635422, -0.84611165, 0.10982452)
COS_C = (1.4142135, -6.97885095, 5.73946038, -1.88355791, 0.31068803)
MAGIC = 12582912.0
TILE_UNROLL = 4


def nn(a, b):
    return lax.dot_general(a, b, (((1,), (0,)), ((), ())), preferred_element_type=F32)


def nt(a, b):
    return lax.dot_general(a, b, (((1,), (1,)), ((), ())), preferred_element_type=F32)


def horner(coefs, u):
    acc = coefs[-1] * u + coefs[-2]
    for c in coefs[-3::-1]:
        acc = acc * u + c
    return acc


def cos_sin_turns(t):
    r = t - ((t + MAGIC) - MAGIC)
    u = r * r
    s = horner(SIN_C, u) * r
    c = horner(COS_C, u)
    return 1.0 - s * s, s * c


def kernel(
    n_dom,
    n_group,
    slots,
    send_s,
    tiles_s,
    count_s,
    tiles_v,
    coords,
    wave,
    feats,
    cot,
    w_rad_a,
    w_rad_b,
    w_charge,
    w_long,
    norm_gain,
    w_in,
    w_out,
    out_feats,
    out_adj,
    coef,
    ya,
    xa,
    wab,
    wave16,
    sbuf,
    halo,
    rbuf,
    rrecv,
    ct,
    cst,
    sacc,
    sbf,
    srecv,
    wg,
    pj,
    kt,
    tacc,
    gacc,
    adj,
    idx_v,
    idx_s,
    idx_sem,
    halo_send,
    halo_recv,
    back_send,
    back_recv,
    rs_send,
    rs_recv,
    ag_send,
    ag_recv,
):
    me = lax.axis_index("dom")
    grp = lax.axis_index("group")
    nblk = feats.shape[0]
    extent = nblk + 4 * HB
    others = n_dom - 1
    dom_next, dom_prev = lax.rem(me + 1, n_dom), lax.rem(me + n_dom - 1, n_dom)
    grp_next, grp_prev = lax.rem(grp + 1, n_group), lax.rem(grp + n_group - 1, n_group)
    forward = ((dom_next, "dom"), (dom_prev, "dom"), (grp_next, "group"), (grp_prev, "group"))
    backward = (forward[1], forward[0], forward[3], forward[2])

    barrier = pltpu.get_barrier_semaphore()

    def greet(o, carry):
        pl.semaphore_signal(
            barrier, inc=1, device_id={"dom": lax.rem(me + o, n_dom)}, device_id_type=MESH
        )
        return carry

    lax.fori_loop(1, n_dom, greet, 0)
    for peer in (grp_next, grp_prev):
        pl.semaphore_signal(barrier, inc=1, device_id={"group": peer}, device_id_type=MESH)

    eye = (
        lax.broadcasted_iota(jnp.int32, (BLK, BLK), 0)
        == lax.broadcasted_iota(jnp.int32, (BLK, BLK), 1)
    ).astype(BF16)

    x = coords[...].astype(F32)
    x2 = x[0:1] * x[0:1] + x[1:2] * x[1:2] + x[2:3] * x[2:3]
    hi = x2.astype(BF16).astype(F32)
    mid = (x2 - hi).astype(BF16).astype(F32)
    lo = x2 - hi - mid
    atoms = nblk * BLK
    coef[0, :, :] = jnp.zeros((16, atoms), F32)
    coef[1, :, :] = jnp.zeros((16, atoms), F32)
    ones = jnp.ones((3, atoms), F32)
    coef[0, 0:3, :] = x
    coef[1, 0:3, :] = -2.0 * x
    for part, value in enumerate((hi, mid, lo)):
        coef[0, 3 + part : 4 + part, :] = value
        coef[1, 6 + part : 7 + part, :] = value
    coef[0, 6:9, :] = ones
    coef[1, 3:6, :] = ones
    for b in range(nblk):
        cols = slice(b * BLK, (b + 1) * BLK)
        ya[b, :, :] = coef[1, :, cols].astype(BF16)
        xa[b, :, :] = nt(eye, coef[0, :, cols].astype(BF16)).astype(BF16)

    for d in range(4):
        for h in range(HB):
            pick = send_s[h, d]
            sbuf[d, h, 0:BLK, :] = feats[pick]
            sbuf[d, h, BLK : BLK + 16, :] = ya[pick]

    sub = lax.broadcasted_iota(jnp.int32, (BLK, BLK), 0)
    lane = lax.broadcasted_iota(jnp.int32, (BLK, BLK), 1)
    lane_row = lax.broadcasted_iota(jnp.int32, (1, BLK), 1)

    def chains(row, live_rows):
        row = jnp.broadcast_to(row, (BLK, BLK))
        col = row.T
        before = (col == row) & (sub < lane)
        prev = jnp.max(jnp.where(before, sub + 1, 0), axis=0, keepdims=True)
        alive = (col == lane) & (sub < live_rows)
        last = jnp.max(jnp.where(alive, sub + 1, 0), axis=0, keepdims=True)
        return prev, last

    idx_v[...] = jnp.full((8, BLK), -1, jnp.int32)
    idx_v[0:2, 0:slots] = tiles_v[...]
    count = count_s[0]
    prev_t, last_t = chains(idx_v[0:1, :], count)
    prev_s, last_s = chains(idx_v[1:2, :], count)
    list_row = jnp.full((1, BLK), -1, jnp.int32)
    for d in range(4):
        for h in range(HB):
            list_row = jnp.where(lane_row == d * HB + h, send_s[h, d], list_row)
    prev_l, last_l = chains(list_row, 4 * HB)
    prev_l = jnp.where(prev_l > 0, prev_l + (nblk - 1), list_row)
    last_l = jnp.where(last_l > 0, last_l + (nblk - 1), lane_row)
    for r, row in enumerate((prev_t, prev_s, last_t, last_s, prev_l, last_l)):
        idx_v[r : r + 1, :] = row
    index_copy = pltpu.make_async_copy(idx_v, idx_s, idx_sem)
    index_copy.start()

    wct = nt(eye, w_charge[...]).astype(BF16)
    wab[:, 0:F] = w_rad_a[...]
    wab[:, F : 2 * F] = w_rad_b[...]
    waves = wave[...].astype(F32)
    n_k = waves.shape[1]
    half = n_k // 2
    wave16[...] = jnp.zeros((16, n_k), F32)
    wave16[0:3, :] = waves

    def local_block(b, carry):
        block = feats[b]
        ct[b] = nt(wct, block).astype(BF16)
        both = nn(block, wab[...]).astype(BF16)
        pj[b, 0:BLK, :] = both[:, 0:F]
        pj[b, BLK : 2 * BLK, :] = both[:, F : 2 * F]
        kt[b] = nt(eye, cot[b]).astype(BF16)
        return carry

    lax.fori_loop(0, nblk, local_block, 0)

    sacc[...] = jnp.zeros_like(sacc)

    def structure(b, carry):
        rows = pl.ds(pl.multiple_of(b * BLK, BLK), BLK)
        left = xa[b]
        for q in range(n_k // BLK):
            turns = nn(left, wave16[:, q * BLK : (q + 1) * BLK].astype(BF16))
            c, s = cos_sin_turns(turns)
            k0 = q * BLK
            base = (k0 // half) * 2 * half + k0 % half
            cst[rows, base : base + BLK] = c.astype(BF16)
            cst[rows, base + half : base + half + BLK] = s.astype(BF16)
        sacc[...] += nn(ct[b], cst[rows, :])
        return carry

    lax.fori_loop(0, nblk // 2, structure, 0)
    pl.semaphore_wait(barrier, others + 2)

    def halo_copy(d, buf, into, ways, send, recv):
        peer, axis = ways[d]
        return pltpu.make_async_remote_copy(
            src_ref=buf.at[d],
            dst_ref=into.at[d],
            send_sem=send.at[d],
            recv_sem=recv.at[d],
            device_id={axis: peer},
            device_id_type=MESH,
        )

    for d in range(4):
        halo_copy(d, sbuf, halo, forward, halo_send, halo_recv).start()

    lax.fori_loop(nblk // 2, nblk, structure, 0)

    for cb in range(4):
        sbf[cb] = sacc[:, cb * half : (cb + 1) * half].astype(BF16)

    rows16 = (4 * F) // n_dom
    per_cb = F // rows16

    def piece(buf, p):
        return buf.at[p // per_cb, pl.ds(pl.multiple_of(lax.rem(p, per_cb) * rows16, rows16), rows16), :]

    def rs_copy(o):
        peer = lax.rem(me + o, n_dom)
        return pltpu.make_async_remote_copy(
            src_ref=piece(sbf, peer),
            dst_ref=srecv.at[o - 1],
            send_sem=rs_send.at[o - 1],
            recv_sem=rs_recv.at[o - 1],
            device_id={"dom": peer},
            device_id_type=MESH,
        )

    def ag_copy(o):
        peer = lax.rem(me + o, n_dom)
        return pltpu.make_async_remote_copy(
            src_ref=piece(wg, me),
            dst_ref=piece(wg, me),
            send_sem=ag_send.at[o - 1],
            recv_sem=ag_recv.at[o - 1],
            device_id={"dom": peer},
            device_id_type=MESH,
        )

    def for_others(do):
        def step(o, carry):
            do(o)
            return carry

        lax.fori_loop(1, n_dom, step, 0)

    for_others(lambda o: rs_copy(o).start())

    index_copy.wait()
    for d in range(4):
        halo_copy(d, sbuf, halo, forward, halo_send, halo_recv).wait()
    for d in range(4):
        for h in range(HB):
            e = nblk + d * HB + h
            ya[e] = halo[d, h, BLK : BLK + 16, :]
            both = nn(halo[d, h, 0:BLK, :], wab[...]).astype(BF16)
            pj[e, 0:BLK, :] = both[:, 0:F]
            pj[e, BLK : 2 * BLK, :] = both[:, F : 2 * F]

    tacc[0] = jnp.zeros((BLK, F), F32)
    gacc[0] = jnp.zeros((F, 2 * BLK), F32)

    def slot(r, t, most):
        return jnp.clip(idx_s[r, t], 0, most)

    def tile(t):
        i = tiles_s[0, t]
        j = tiles_s[1, t]
        dist2 = nn(xa[i], ya[j])
        ka = jnp.exp2(dist2 * (-6.0 * LOG2E))
        k2 = ka * ka
        kb = (k2 * k2) * ka
        kk = jnp.concatenate([ka.astype(BF16), kb.astype(BF16)], axis=1)
        tacc[t + 1] = tacc[slot(0, t, slots)] + nn(kk, pj[j])
        gacc[t + 1] = gacc[slot(1, t, slots)] + nn(kt[i], kk)

    def tile_step(step, carry):
        for u in range(TILE_UNROLL):
            tile(step * TILE_UNROLL + u)
        return carry

    steps = slots // TILE_UNROLL
    lax.fori_loop(0, steps // 2, tile_step, 0)

    for_others(lambda o: rs_copy(o).wait_recv())
    row_cb = me // per_cb
    row_in = pl.multiple_of(lax.rem(me, per_cb) * rows16, rows16)
    total = sbf[row_cb, pl.ds(row_in, rows16), :].astype(F32)
    total = total + jnp.sum(srecv[...].astype(F32), axis=0)
    norm2 = waves[0:1] * waves[0:1] + waves[1:2] * waves[1:2] + waves[2:3] * waves[2:3]
    strength = jnp.exp(norm2 * (-1.0 / 16.0)) / (1.0 + norm2) * float(atoms * n_dom) ** (-0.5)
    strength = jnp.where(me // (2 * per_cb) == 0, strength[:, 0:half], strength[:, half : 2 * half])
    wg[row_cb, pl.ds(row_in, rows16), :] = (total * strength).astype(BF16)
    for_others(lambda o: ag_copy(o).start())

    lax.fori_loop(steps // 2, steps, tile_step, 0)

    def grad_block(e):
        g = (gacc[slot(3, e, slots)] * SCALE).astype(BF16)
        rows = jnp.concatenate([nt(eye, g[:, 0:BLK]), nt(eye, g[:, BLK : 2 * BLK])], axis=1)
        return nt(rows.astype(BF16), wab[...])

    for d in range(4):
        for h in range(HB):
            rbuf[d, h] = grad_block(nblk + d * HB + h).astype(BF16)
    for d in range(4):
        halo_copy(d, rbuf, rrecv, backward, back_send, back_recv).start()

    def own_grad(b, carry):
        adj[b] = grad_block(b)
        return carry

    lax.fori_loop(0, nblk, own_grad, 0)

    for_others(lambda o: ag_copy(o).wait_recv())

    gain = norm_gain[...]

    def update(b, carry):
        pot = None
        for cb in range(4):
            rows = pl.ds(pl.multiple_of(b * 2 * BLK, 2 * BLK), 2 * BLK)
            term = nt(cst[rows, cb * half : (cb + 1) * half], wg[cb])
            pot = term if pot is None else pot + term
        long_msg = nn(pot.astype(BF16), w_long[...])
        msg = jnp.concatenate([tacc[slot(2, 2 * b, slots)], tacc[slot(2, 2 * b + 1, slots)]], axis=0) * SCALE
        own = jnp.concatenate([feats[2 * b], feats[2 * b + 1]], axis=0).astype(F32)
        mixed = own + msg + long_msg
        scale = lax.rsqrt(jnp.mean(mixed * mixed, axis=1, keepdims=True) + 1e-06)
        normed = (mixed * scale * gain).astype(BF16)
        pre = nn(normed, w_in[...])
        hidden = (pre * (0.5 + 0.5 * jnp.tanh(0.5 * pre))).astype(BF16)
        new = (mixed + nn(hidden, w_out[...])).astype(BF16)
        out_feats[2 * b] = new[0:BLK]
        out_feats[2 * b + 1] = new[BLK : 2 * BLK]
        return carry

    lax.fori_loop(0, nblk // 2, update, 0)

    for d in range(4):
        halo_copy(d, rbuf, rrecv, backward, back_send, back_recv).wait()
    for k in range(4 * HB):
        adj[nblk + k] = adj[slot(4, k, extent - 1)] + rrecv[k // HB, k % HB].astype(F32)

    def finish(b, carry):
        out_adj[b] = adj[slot(5, b, extent - 1)]
        return carry

    lax.fori_loop(0, nblk, finish, 0)
    for_others(lambda o: rs_copy(o).wait_send())
    for_others(lambda o: ag_copy(o).wait_send())


def solution(mesh):
    n_dom, n_group = mesh.shape["dom"], mesh.shape["group"]

    def body(
        feats,
        coords,
        msg_cot,
        send_list,
        tiles,
        tile_count,
        wavevec,
        w_rad_a,
        w_rad_b,
        w_charge,
        w_long,
        norm_gain,
        w_in,
        w_out,
    ):
        atoms = feats.shape[0]
        nblk = atoms // BLK
        extent = nblk + 4 * HB
        slots = tiles.shape[1]
        n_k = wavevec.shape[0]
        half = n_k // 2
        rows16 = (4 * F) // n_dom
        vmem = pl.BlockSpec(memory_space=pltpu.VMEM)
        smem = pl.BlockSpec(memory_space=pltpu.SMEM)
        tiles_t = tiles[0].T
        dma = pltpu.SemaphoreType.DMA
        new_feats, adjoint = pl.pallas_call(
            functools.partial(kernel, n_dom, n_group, slots),
            out_shape=(
                jax.ShapeDtypeStruct((nblk, BLK, F), BF16),
                jax.ShapeDtypeStruct((nblk, BLK, F), F32),
            ),
            in_specs=[smem, smem, smem] + [vmem] * 12,
            out_specs=(vmem, vmem),
            scratch_shapes=[
                pltpu.VMEM((2, 16, atoms), F32),
                pltpu.VMEM((extent, 16, BLK), BF16),
                pltpu.VMEM((nblk, BLK, 16), BF16),
                pltpu.VMEM((F, 2 * F), BF16),
                pltpu.VMEM((16, n_k), F32),
                pltpu.VMEM((4, HB, BLK + 16, F), BF16),
                pltpu.VMEM((4, HB, BLK + 16, F), BF16),
                pltpu.VMEM((4, HB, BLK, F), BF16),
                pltpu.VMEM((4, HB, BLK, F), BF16),
                pltpu.VMEM((nblk, F, BLK), BF16),
                pltpu.VMEM((atoms, 2 * n_k), BF16),
                pltpu.VMEM((F, 2 * n_k), F32),
                pltpu.VMEM((4, F, half), BF16),
                pltpu.VMEM((n_dom - 1, rows16, half), BF16),
                pltpu.VMEM((4, F, half), BF16),
                pltpu.VMEM((extent, 2 * BLK, F), BF16),
                pltpu.VMEM((nblk, F, BLK), BF16),
                pltpu.VMEM((slots + 1, BLK, F), F32),
                pltpu.VMEM((slots + 1, F, 2 * BLK), F32),
                pltpu.VMEM((extent, BLK, F), F32),
                pltpu.VMEM((8, BLK), jnp.int32),
                pltpu.SMEM((8, BLK), jnp.int32),
                dma,
                dma((4,)),
                dma((4,)),
                dma((4,)),
                dma((4,)),
                dma((n_dom - 1,)),
                dma((n_dom - 1,)),
                dma((n_dom - 1,)),
                dma((n_dom - 1,)),
            ],
            compiler_params=pltpu.CompilerParams(
                collective_id=0, has_side_effects=True, vmem_limit_bytes=58 << 20
            ),
        )(
            send_list[0].T,
            tiles_t,
            tile_count,
            tiles_t,
            coords,
            wavevec.T,
            feats.reshape(nblk, BLK, F),
            msg_cot.reshape(nblk, BLK, F),
            w_rad_a,
            w_rad_b,
            w_charge,
            w_long,
            norm_gain.reshape(1, F),
            w_in,
            w_out,
        )
        return new_feats.reshape(atoms, F), adjoint.reshape(atoms, F)

    return jax.shard_map(
        body,
        mesh=mesh,
        in_specs=(
            P(("group", "dom"), None),
            P(None, ("group", "dom")),
            P(("group", "dom"), None),
            P(("group", "dom"), None, None),
            P(("group", "dom"), None, None),
            P(("group", "dom")),
            P(),
            P(),
            P(),
            P(),
            P(),
            P(),
            P(),
            P(),
        ),
        out_specs=(P(("group", "dom"), None), P(("group", "dom"), None)),
        check_vma=False,
    )
```

time: 244 us -> 62.9 us (0.26); the launches traced: 239 us -> 62.8 us
  matrix products: 110 us -> 0 us
  starting transfers between devices: 70 us -> 0 us
  Pallas kernels: 0 us -> 58.6 us
  local copies, waits for them, and re-layouts: 26.1 us -> 2.93 us
  other arithmetic: 12.5 us -> 0 us
  waiting for transfers between devices: 10.6 us -> 0 us
  loops' own time: 8.02 us -> 0 us
    dot_general x67 -> x0, matrix products: 110 us -> none  [the longest x1 16.6 us: body(): jnp.dot(potential.astype(jnp.bfloat16), w_long, preferred_element_type=jn...]
    pallas_call x0 -> x1, Pallas kernels: none -> 58.6 us  [body(): pl.pallas_call(functools.partial(kernel, n_dom, n_group, slots), out_shap...]
    all_to_all x2 -> x0, starting transfers between devices: 47.9 us -> none  [the longest x1 36.9 us: from_everyone(): return lax.all_to_all(copies, axis, split_axis=0, concat_axis=0, tiled=True)]
    ppermute x12 -> x0, starting transfers between devices: 22.1 us -> none  [passed_along(): lax.ppermute(shard, axis, [(i, (i + by) % length) for i in range(length)])]
    another operation x7 -> x0, loops' own time: 8.02 us -> none  [the longest x1 7.37 us: body(): lax.scan(tile_step, start, jnp.arange(slots // TILE_STEP, dtype=jnp.int32))]
    all_to_all x2 -> x0, waiting for transfers between devices: 7.47 us -> none  [the longest x1 7.46 us: from_everyone(): return lax.all_to_all(copies, axis, split_axis=0, concat_axis=0, tiled=True)]
    cond x40 -> x0, local copies, waits for them, and re-layouts: 7.06 us -> none
    convert_element_type x9 -> x0, other arithmetic: 5.34 us -> none  [the longest x6 3.9 us: body(): live_all = (jnp.arange(slots) < count).astype(jnp.float32)]
  transfers between devices with their start and end apart: 14 -> 0, of which waited for: 2 -> 0; matrix products, arithmetic and copies ran while one was open for 44% -> 0% of each run, Pallas kernels for 0% -> 0%
where the time goes in v1:
time: 62.9 us; the launch traced here: 62.8 us
  Pallas kernels  58.6 us (93%)
  local copies, waits for them, and re-layouts  2.93 us (5%)
  between operations  1.3 us (2%)
    pallas_call x1, Pallas kernels, body(): pl.pallas_call(functools.partial(kernel, n_dom, n_group, slots), out_shap...  58.6 us
    unnamed x4, local copies, waits for them, and re-layouts  2.93 us

profile of v1, /device:TPU:1, one launch (start us, length us, event | category | flops | bytes accessed | tf_op | source)
XLA Modules:
  0.0 62.8 jit_solution(6628545973870046105)
XLA Ops:
  1.3 58.6 %shard_map.149 = (bf16[16,128,128]{2,1,0:T(8,128)(2,1)}, f32[16,128,128]{2,1,0:T(8,128)}) custom-call(s32[2,4]{1,0:T(2,128)} %bitcast.19, s32[2,96]{1,0:T(2,128)} %bitcast.17, s32[1]{0:T(128)S(6)} %copy.18.count_s, s32[2,96]{1,0:T(2,128)} %bitcast.18, bf16[3,2048]{1,0:T(4,128)(2,1)} %coords.1, s32[3,512]{1,0:T(4,128)} %bitcast.16, ...), custom_call_target="tpu_custom_call" | custom-call | tf_op jit(solution)/shard_map/pallas_call | solution.py:413
  59.9 0.0 copy-start
  59.9 2.0 %copy.19 = bf16[2048,128]{1,0:T(8,128)(2,1)} copy(bf16[2048,128]{1,0:T(8,128)(2,1)} %bitcast.13) | data formatting | bytes 1048576
  61.8 0.0 copy-done
  61.8 1.0 %copy.20 = f32[2048,128]{1,0:T(8,128)} copy(f32[2048,128]{1,0:T(8,128)S(1)} %bitcast.12) | data formatting | bytes 2097152
Async XLA Ops:
  59.9 2.0 %copy-start = (f32[16,128,128]{2,1,0:T(8,128)S(1)}, f32[16,128,128]{2,1,0:T(8,128)}, u32[]{:S(2)}) copy-start(f32[16,128,128]{2,1,0:T(8,128)} %get-tuple-element.5) | copy-start | bytes 3145732

commit v2 on v1

--- a/solution.py
+++ b/solution.py
@@ -18,7 +18,8 @@
 SIN_C = (4.44288292, -7.30824569, 3.60635422, -0.84611165, 0.10982452)
 COS_C = (1.4142135, -6.97885095, 5.73946038, -1.88355791, 0.31068803)
 MAGIC = 12582912.0
-TILE_UNROLL = 4
+GROUP = 4
+CHUNK = 4
 
 
 def nn(a, b):
@@ -74,7 +75,6 @@
     halo,
     rbuf,
     rrecv,
-    ct,
     cst,
     sacc,
     sbf,
@@ -85,6 +85,9 @@
     tacc,
     gacc,
     adj,
+    keven,
+    kodd,
+    wgt,
     idx_v,
     idx_s,
     idx_sem,
@@ -143,7 +146,11 @@
     for b in range(nblk):
         cols = slice(b * BLK, (b + 1) * BLK)
         ya[b, :, :] = coef[1, :, cols].astype(BF16)
-        xa[b, :, :] = nt(eye, coef[0, :, cols].astype(BF16)).astype(BF16)
+        aug = coef[0, :, cols].astype(BF16)
+        pad = jnp.zeros((16, BLK), BF16)
+        turned = nt(eye, jnp.concatenate([aug, pad, pad, aug], axis=0)).astype(BF16)
+        xa[0, b, :, :] = turned[:, 0:32]
+        xa[1, b, :, :] = turned[:, 32:64]
 
     for d in range(4):
         for h in range(HB):
@@ -187,36 +194,36 @@
     waves = wave[...].astype(F32)
     n_k = waves.shape[1]
     half = n_k // 2
-    wave16[...] = jnp.zeros((16, n_k), F32)
+    wave16[...] = jnp.zeros((32, n_k), F32)
     wave16[0:3, :] = waves
 
-    def local_block(b, carry):
-        block = feats[b]
-        ct[b] = nt(wct, block).astype(BF16)
-        both = nn(block, wab[...]).astype(BF16)
-        pj[b, 0:BLK, :] = both[:, 0:F]
-        pj[b, BLK : 2 * BLK, :] = both[:, F : 2 * F]
-        kt[b] = nt(eye, cot[b]).astype(BF16)
+    sacc[...] = jnp.zeros_like(sacc)
+
+    def structure(step, carry):
+        first = step * 2
+        pair = feats[pl.ds(first, 2)].reshape(2 * BLK, F)
+        both = nn(pair, wab[...]).astype(BF16)
+        for sub_b in range(2):
+            here = slice(sub_b * BLK, (sub_b + 1) * BLK)
+            pj[first + sub_b, 0:BLK, :] = both[here, 0:F]
+            pj[first + sub_b, BLK : 2 * BLK, :] = both[here, F : 2 * F]
+            kt[first + sub_b] = nt(eye, cot[first + sub_b]).astype(BF16)
+        charges = nt(wct, pair).astype(BF16)
+        for sub_b in range(2):
+            left = xa[0, first + sub_b]
+            rows = pl.ds(pl.multiple_of((first + sub_b) * BLK, BLK), BLK)
+            for q in range(n_k // BLK):
+                turns = nn(left, wave16[:, q * BLK : (q + 1) * BLK].astype(BF16))
+                c, s = cos_sin_turns(turns)
+                k0 = q * BLK
+                base = (k0 // half) * 2 * half + k0 % half
+                cst[rows, base : base + BLK] = c.astype(BF16)
+                cst[rows, base + half : base + half + BLK] = s.astype(BF16)
+        two_rows = pl.ds(pl.multiple_of(first * BLK, 2 * BLK), 2 * BLK)
+        sacc[...] += nn(charges, cst[two_rows, :])
         return carry
 
-    lax.fori_loop(0, nblk, local_block, 0)
-
-    sacc[...] = jnp.zeros_like(sacc)
-
-    def structure(b, carry):
-        rows = pl.ds(pl.multiple_of(b * BLK, BLK), BLK)
-        left = xa[b]
-        for q in range(n_k // BLK):
-            turns = nn(left, wave16[:, q * BLK : (q + 1) * BLK].astype(BF16))
-            c, s = cos_sin_turns(turns)
-            k0 = q * BLK
-            base = (k0 // half) * 2 * half + k0 % half
-            cst[rows, base : base + BLK] = c.astype(BF16)
-            cst[rows, base + half : base + half + BLK] = s.astype(BF16)
-        sacc[...] += nn(ct[b], cst[rows, :])
-        return carry
-
-    lax.fori_loop(0, nblk // 2, structure, 0)
+    lax.fori_loop(0, nblk // 4, structure, 0)
     pl.semaphore_wait(barrier, others + 2)
 
     def halo_copy(d, buf, into, ways, send, recv):
@@ -233,7 +240,7 @@
     for d in range(4):
         halo_copy(d, sbuf, halo, forward, halo_send, halo_recv).start()
 
-    lax.fori_loop(nblk // 2, nblk, structure, 0)
+    lax.fori_loop(nblk // 4, nblk // 2, structure, 0)
 
     for cb in range(4):
         sbf[cb] = sacc[:, cb * half : (cb + 1) * half].astype(BF16)
@@ -292,23 +299,44 @@
     def slot(r, t, most):
         return jnp.clip(idx_s[r, t], 0, most)
 
-    def tile(t):
-        i = tiles_s[0, t]
-        j = tiles_s[1, t]
-        dist2 = nn(xa[i], ya[j])
-        ka = jnp.exp2(dist2 * (-6.0 * LOG2E))
-        k2 = ka * ka
-        kb = (k2 * k2) * ka
-        kk = jnp.concatenate([ka.astype(BF16), kb.astype(BF16)], axis=1)
-        tacc[t + 1] = tacc[slot(0, t, slots)] + nn(kk, pj[j])
-        gacc[t + 1] = gacc[slot(1, t, slots)] + nn(kt[i], kk)
+    def make_kernels(buf, group):
+        group = jnp.minimum(group, groups - 1)
+        zero = jnp.zeros((16, BLK), BF16)
+        for u in range(0, GROUP, 2):
+            t = group * GROUP + u
+            left = xa[0, tiles_s[0, t]] + xa[1, tiles_s[0, t + 1]]
+            top = jnp.concatenate([ya[tiles_s[1, t]], zero], axis=1)
+            low = jnp.concatenate([zero, ya[tiles_s[1, t + 1]]], axis=1)
+            dist2 = nn(left, jnp.concatenate([top, low], axis=0))
+            ka = jnp.exp2(dist2 * (-6.0 * LOG2E))
+            k2 = ka * ka
+            kb = (k2 * k2) * ka
+            ka = ka.astype(BF16)
+            kb = kb.astype(BF16)
+            for v in range(2):
+                here = slice(v * BLK, (v + 1) * BLK)
+                buf[u + v, :, 0:BLK] = ka[:, here]
+                buf[u + v, :, BLK : 2 * BLK] = kb[:, here]
+
+    def use_kernels(buf, group):
+        for u in range(GROUP):
+            t = group * GROUP + u
+            kk = buf[u]
+            term = nn(kk, pj[tiles_s[1, t]])
+            back = nn(kt[tiles_s[0, t]], kk)
+            tacc[t + 1] = tacc[slot(0, t, slots)] + term
+            gacc[t + 1] = gacc[slot(1, t, slots)] + back
 
     def tile_step(step, carry):
-        for u in range(TILE_UNROLL):
-            tile(step * TILE_UNROLL + u)
+        make_kernels(kodd, 2 * step + 1)
+        use_kernels(keven, 2 * step)
+        make_kernels(keven, 2 * step + 2)
+        use_kernels(kodd, 2 * step + 1)
         return carry
 
-    steps = slots // TILE_UNROLL
+    groups = slots // GROUP
+    steps = groups // 2
+    make_kernels(keven, 0)
     lax.fori_loop(0, steps // 2, tile_step, 0)
 
     for_others(lambda o: rs_copy(o).wait_recv())
@@ -326,8 +354,7 @@
 
     def grad_block(e):
         g = (gacc[slot(3, e, slots)] * SCALE).astype(BF16)
-        rows = jnp.concatenate([nt(eye, g[:, 0:BLK]), nt(eye, g[:, BLK : 2 * BLK])], axis=1)
-        return nt(rows.astype(BF16), wab[...])
+        return nn(wab[...], jnp.concatenate([g[:, 0:BLK], g[:, BLK : 2 * BLK]], axis=0))
 
     for d in range(4):
         for h in range(HB):
@@ -345,26 +372,35 @@
 
     gain = norm_gain[...]
 
-    def update(b, carry):
+    wide_eye = (
+        lax.broadcasted_iota(jnp.int32, (half, half), 0)
+        == lax.broadcasted_iota(jnp.int32, (half, half), 1)
+    ).astype(BF16)
+    for cb in range(4):
+        wgt[cb] = nt(wide_eye, wg[cb]).astype(BF16)
+
+    def update(step, carry):
+        rows = pl.ds(pl.multiple_of(step * CHUNK * BLK, CHUNK * BLK), CHUNK * BLK)
         pot = None
         for cb in range(4):
-            rows = pl.ds(pl.multiple_of(b * 2 * BLK, 2 * BLK), 2 * BLK)
-            term = nt(cst[rows, cb * half : (cb + 1) * half], wg[cb])
+            term = nn(cst[rows, cb * half : (cb + 1) * half], wgt[cb])
             pot = term if pot is None else pot + term
         long_msg = nn(pot.astype(BF16), w_long[...])
-        msg = jnp.concatenate([tacc[slot(2, 2 * b, slots)], tacc[slot(2, 2 * b + 1, slots)]], axis=0) * SCALE
-        own = jnp.concatenate([feats[2 * b], feats[2 * b + 1]], axis=0).astype(F32)
-        mixed = own + msg + long_msg
+        first = step * CHUNK
+        msg = jnp.concatenate(
+            [tacc[slot(2, first + v, slots)] for v in range(CHUNK)], axis=0
+        )
+        own = feats[pl.ds(first, CHUNK)].reshape(CHUNK * BLK, F).astype(F32)
+        mixed = own + msg * SCALE + long_msg
         scale = lax.rsqrt(jnp.mean(mixed * mixed, axis=1, keepdims=True) + 1e-06)
         normed = (mixed * scale * gain).astype(BF16)
         pre = nn(normed, w_in[...])
         hidden = (pre * (0.5 + 0.5 * jnp.tanh(0.5 * pre))).astype(BF16)
         new = (mixed + nn(hidden, w_out[...])).astype(BF16)
-        out_feats[2 * b] = new[0:BLK]
-        out_feats[2 * b + 1] = new[BLK : 2 * BLK]
+        out_feats[pl.ds(first, CHUNK)] = new.reshape(CHUNK, BLK, F)
         return carry
 
-    lax.fori_loop(0, nblk // 2, update, 0)
+    lax.fori_loop(0, nblk // CHUNK, update, 0)
 
     for d in range(4):
         halo_copy(d, rbuf, rrecv, backward, back_send, back_recv).wait()
@@ -372,7 +408,7 @@
         adj[nblk + k] = adj[slot(4, k, extent - 1)] + rrecv[k // HB, k % HB].astype(F32)
 
     def finish(b, carry):
-        out_adj[b] = adj[slot(5, b, extent - 1)]
+        out_adj[b] = adj[slot(5, b, extent - 1)].T
         return carry
 
     lax.fori_loop(0, nblk, finish, 0)
@@ -421,14 +457,13 @@
             scratch_shapes=[
                 pltpu.VMEM((2, 16, atoms), F32),
                 pltpu.VMEM((extent, 16, BLK), BF16),
-                pltpu.VMEM((nblk, BLK, 16), BF16),
+                pltpu.VMEM((2, nblk, BLK, 32), BF16),
                 pltpu.VMEM((F, 2 * F), BF16),
-                pltpu.VMEM((16, n_k), F32),
+                pltpu.VMEM((32, n_k), F32),
                 pltpu.VMEM((4, HB, BLK + 16, F), BF16),
                 pltpu.VMEM((4, HB, BLK + 16, F), BF16),
                 pltpu.VMEM((4, HB, BLK, F), BF16),
                 pltpu.VMEM((4, HB, BLK, F), BF16),
-                pltpu.VMEM((nblk, F, BLK), BF16),
                 pltpu.VMEM((atoms, 2 * n_k), BF16),
                 pltpu.VMEM((F, 2 * n_k), F32),
                 pltpu.VMEM((4, F, half), BF16),
@@ -438,7 +473,10 @@
                 pltpu.VMEM((nblk, F, BLK), BF16),
                 pltpu.VMEM((slots + 1, BLK, F), F32),
                 pltpu.VMEM((slots + 1, F, 2 * BLK), F32),
-                pltpu.VMEM((extent, BLK, F), F32),
+                pltpu.VMEM((extent, F, BLK), F32),
+                pltpu.VMEM((GROUP, BLK, 2 * BLK), BF16),
+                pltpu.VMEM((GROUP, BLK, 2 * BLK), BF16),
+                pltpu.VMEM((4, half, F), BF16),
                 pltpu.VMEM((8, BLK), jnp.int32),
                 pltpu.SMEM((8, BLK), jnp.int32),
                 dma,

time: 62.9 us -> 48.7 us (0.77)
  Pallas kernels: 58.6 us -> 44.4 us
    pallas_call x1, Pallas kernels: 58.6 us -> 44.4 us  [body(): pl.pallas_call(functools.partial(kernel, n_dom, n_group, slots), out_shap...]
where the time goes in v2:
time: 48.7 us; the launch traced here: 48.6 us
  Pallas kernels  44.4 us (91%)
  local copies, waits for them, and re-layouts  2.93 us (6%)
  between operations  1.3 us (3%)
    pallas_call x1, Pallas kernels, body(): pl.pallas_call(functools.partial(kernel, n_dom, n_group, slots), out_shap...  44.4 us
    unnamed x4, local copies, waits for them, and re-layouts  2.93 us

profile of v2, /device:TPU:1, one launch (start us, length us, event | category | flops | bytes accessed | tf_op | source)
XLA Modules:
  0.0 48.6 jit_solution(26798731006025297)
XLA Ops:
  1.3 44.4 %shard_map.149 = (bf16[16,128,128]{2,1,0:T(8,128)(2,1)}, f32[16,128,128]{2,1,0:T(8,128)}) custom-call(s32[2,4]{1,0:T(2,128)} %bitcast.19, s32[2,96]{1,0:T(2,128)} %bitcast.17, s32[1]{0:T(128)S(6)} %copy.18.count_s, s32[2,96]{1,0:T(2,128)} %bitcast.18, bf16[3,2048]{1,0:T(4,128)(2,1)} %coords.1, s32[3,512]{1,0:T(4,128)} %bitcast.16, ...), custom_call_target="tpu_custom_call" | custom-call | tf_op jit(solution)/shard_map/pallas_call | solution.py:449
  45.6 0.0 copy-start
  45.6 2.0 %copy.19 = bf16[2048,128]{1,0:T(8,128)(2,1)} copy(bf16[2048,128]{1,0:T(8,128)(2,1)} %bitcast.13) | data formatting | bytes 1048576
  47.6 0.0 copy-done
  47.6 1.0 %copy.20 = f32[2048,128]{1,0:T(8,128)} copy(f32[2048,128]{1,0:T(8,128)S(1)} %bitcast.12) | data formatting | bytes 2097152
Async XLA Ops:
  45.6 2.0 %copy-start = (f32[16,128,128]{2,1,0:T(8,128)S(1)}, f32[16,128,128]{2,1,0:T(8,128)}, u32[]{:S(2)}) copy-start(f32[16,128,128]{2,1,0:T(8,128)} %get-tuple-element.5) | copy-start | bytes 3145732
